TPU v7x, 32 devices: a whole 2x2x4 slice. The times are simulated.
32 devices in a mesh: ctx: 8 (over y, x, core), dp: 4 (over z).
Axes of the slice: x: 2, y: 2, z: 4, core: 2. Of those that a mesh axis runs over, the one named last changes fastest.
Arguments:
- ids: int32 [3072], P('ctx'), may hold values from 0 to 511
- embed_table: bfloat16 [512, 4096], P(None, 'dp'), may hold values from -6 to 6
- norm_gain: bfloat16 [4096], P('dp'), may hold values from 0.25 to 1.75
- w_query: bfloat16 [4096, 4096], P('ctx', 'dp'), may hold values from -0.09375 to 0.09375
- w_key: bfloat16 [4096, 4096], P('ctx', 'dp'), may hold values from -0.09375 to 0.09375
- w_value: bfloat16 [4096, 4096], P('ctx', 'dp'), may hold values from -0.09375 to 0.09375
- short_filter: float32 [3, 3, 4096], P(None, None, 'dp'), may hold values from -4 to 4
- pole_rate: float32 [4096, 16], P('dp'), may hold values from 1.6276042e-05 to 0.05
- residue: float32 [4096, 16], P('dp'), may hold values from -2 to 2
- skip_gain: float32 [4096], P('dp'), may hold values from -4 to 4
- w_out: bfloat16 [4096, 4096], P('ctx', 'dp'), may hold values from -0.09375 to 0.09375
Outputs:
- block_out: bfloat16 [3072, 4096], P('ctx', 'dp')
All inputs are finite; a program needn't handle non-finite values.
Results may differ from a plain program's by a relative error of at most 0.0082.
Values may be sent and summed in bfloat16 or wider, within the bound.
A program may use at most 128 MiB of HBM per device.

v0:
```python
import math

import jax
import jax.numpy as jnp
from jax import lax
from jax.sharding import PartitionSpec as P


def shifted(value, axis, steps):
    count = lax.axis_size(axis)
    initial, last = (max(0, -steps), min(count, count - steps))
    return lax.ppermute(value, axis, [(source, source + steps) for source in range(initial, last)])


def entering_2(value, axis, combine, identity):
    peers, index = (lax.axis_size(axis), lax.axis_index(axis))
    everything = jax.tree.map(lambda part: lax.all_gather(part, axis), value)
    start = jax.tree.map(
        lambda part, zero: jnp.broadcast_to(jnp.asarray(zero, part.dtype), part.shape),
        value,
        identity,
    )

    def turn(k, before):
        reached = k < index
        new = combine(before, jax.tree.map(lambda part: part[k], everything))
        return jax.tree.map(lambda a, b: jnp.where(reached, a, b), new, before)

    return lax.fori_loop(0, peers, turn, start)


def shards(
    ids,
    embed_table,
    norm_gain,
    w_query,
    w_key,
    w_value,
    short_filter,
    pole_rate,
    residue,
    skip_gain,
    w_out,
):
    highest = lax.Precision.HIGHEST
    vocab = embed_table.shape[0]
    channels = w_query.shape[1]
    one_hot = (ids[:, None] == jnp.arange(vocab, dtype=jnp.int32)[None, :]).astype(jnp.bfloat16)
    embedded = jnp.dot(one_hot, embed_table, preferred_element_type=jnp.float32).astype(
        jnp.bfloat16
    )
    full_rows, full_gain = (
        lax.all_gather(embedded, "dp", axis=1, tiled=True),
        lax.all_gather(norm_gain, "dp", axis=0, tiled=True),
    )
    floated = full_rows.astype(jnp.float32)
    scale = lax.rsqrt(jnp.mean(floated * floated, axis=1, keepdims=True) + 1e-06)
    normed = (floated * scale * full_gain.astype(jnp.float32)[None, :]).astype(jnp.bfloat16)
    tok_rows = normed.shape[0]

    def add_rows(piece):
        return jnp.dot(normed, piece, preferred_element_type=jnp.float32)

    query_proj = add_rows(lax.all_gather(w_query, "ctx", axis=0, tiled=True))
    key_proj = add_rows(lax.all_gather(w_key, "ctx", axis=0, tiled=True))
    value_proj = add_rows(lax.all_gather(w_value, "ctx", axis=0, tiled=True))
    projected = jnp.concatenate([query_proj, key_proj, value_proj], axis=1).astype(jnp.bfloat16)
    taps = short_filter.shape[0]
    previous = shifted(projected[tok_rows - (taps - 1) :], "ctx", 1)
    extended = jnp.concatenate([previous, projected], axis=0).astype(jnp.float32)
    filt_rows = short_filter.reshape(taps, 3 * channels)
    convolved = jnp.zeros((tok_rows, 3 * channels), jnp.float32)
    for tap in range(taps):
        convolved = (
            convolved
            + filt_rows[tap][None, :] * extended[taps - 1 - tap : taps - 1 - tap + tok_rows]
        )
    query_conv = convolved[:, :channels]
    gated = convolved[:, channels : 2 * channels] * convolved[:, 2 * channels :]
    sub_len = math.gcd(tok_rows, 64)
    blocks = tok_rows // sub_len
    lag_index = jnp.arange(sub_len, dtype=jnp.int32)
    lags = lag_index.astype(jnp.float32)
    strength = residue * jnp.sqrt(2.0 * pole_rate)
    kernel = jnp.einsum(
        "lck,ck->lc", jnp.exp(-pole_rate[None] * lags[:, None, None]), strength, precision=highest
    )
    offsets = lag_index[:, None] - lag_index[None, :]
    toeplitz = jnp.where((offsets >= 0)[:, :, None], kernel[jnp.maximum(offsets, 0)], 0.0)
    pieces = gated.reshape(blocks, sub_len, channels)
    inside = jnp.einsum("tsc,bsc->btc", toeplitz, pieces, precision=highest)
    tail_decay = jnp.exp(-pole_rate[None] * (sub_len - 1.0 - lags)[:, None, None])
    block_ends = jnp.einsum("sck,bsc->bck", tail_decay, pieces, precision=highest)
    step_decay = jnp.exp(-pole_rate * float(sub_len))

    def advance(state, block_end):
        return (step_decay * state + block_end, state)

    device_end, entering = lax.scan(advance, jnp.zeros_like(step_decay), block_ends)
    device_decay = jnp.exp(-pole_rate * float(tok_rows))

    def combine(earlier, later):
        return (earlier[0] * later[0], later[0] * earlier[1] + later[1])

    decay_total, incoming = entering_2(
        (device_decay, device_end),
        "ctx",
        combine,
        (jnp.ones_like(device_decay), jnp.zeros_like(device_end)),
    )
    block_pos = jnp.arange(blocks, dtype=jnp.float32) * float(sub_len)
    states_in = entering + jnp.exp(-pole_rate[None] * block_pos[:, None, None]) * incoming[None]
    lead = jnp.exp(-pole_rate[None] * (lags + 1.0)[:, None, None]) * strength[None]
    carried = jnp.einsum("tck,bck->btc", lead, states_in, precision=highest)
    long_conv = (inside + carried).reshape(tok_rows, channels) + skip_gain[None, :] * gated
    mixed = (query_conv * long_conv).astype(jnp.bfloat16)
    all_mixed = lax.all_gather(mixed, "dp", axis=1, tiled=True)
    output = jnp.dot(
        all_mixed,
        lax.all_gather(w_out, "ctx", axis=0, tiled=True),
        preferred_element_type=jnp.float32,
    )
    return (embedded.astype(jnp.float32) + output).astype(jnp.bfloat16)


def solution(mesh):
    placed = (
        P("ctx"),
        P(None, "dp"),
        P("dp"),
        P("ctx", "dp"),
        P("ctx", "dp"),
        P("ctx", "dp"),
        P(None, None, "dp"),
        P("dp", None),
        P("dp", None),
        P("dp"),
        P("ctx", "dp"),
    )
    return jax.shard_map(
        shards, mesh=mesh, in_specs=placed, out_specs=P("ctx", "dp"), check_vma=False
    )
```

profile of v0, /device:TPU:0, one launch (start us, length us, event | category | flops | bytes accessed | tf_op | source)
XLA Modules:
  0.0 511.5 jit_solution(16965274444478616923)
XLA Ops:
  6.6 1.2 copy-done
  7.8 2.2 convolution_convert_fusion.3
  10.0 0.7 all-gather.15.cloned.1.call-update
  10.8 0.7 all-gather.13.cloned.1.call-update
  11.5 0.5 all-gather.11.cloned.1.call-update
  12.1 0.5 all-gather.19.cloned.1.call-update
  13.3 12.5 %multiply_reduce_fusion = f32[1024,64]{1,0:T(8,128)} fusion(f32[1024,16]{1,0:T(8,128)S(1)} %copy.47, f32[64]{0:T(128)S(1)} %iota_convert_fusion, f32[1024,16]{1,0:T(8,128)S(1)} %copy.30), kind=kLoop, calls=%fused_computation.14 | loop fusion | flops 3080192 | bytes 393472
  25.9 14.8 %all_gather.34 = bf16[4096]{0:T(1024)(128)(2,1)S(1)} all-gather(bf16[1024]{0:T(1024)(128)(2,1)S(1)} %copy-done.12), channel_id=1, replica_groups=mesh['ctx'=8,'dp'=4] {'dp'}, dimensions={0}, use_global_device_ids=true | all-gather | bytes 10240 | tf_op jit(solution)/shard_map/all_gather | solution.py:54
  40.7 10.9 %all-gather = f32[8192,16]{0,1:T(8,128)} all-gather(f32[1024,16]{0,1:T(8,128)S(1)} %get-tuple-element.213), channel_id=2, replica_groups=mesh['ctx'=8,'dp'=4] {'ctx'}, dimensions={0}, use_global_device_ids=true | all-gather | bytes 589824 | tf_op jit(solution)/shard_map/all_gather | solution.py:17
  51.6 24.7 %all-gather.9.cloned.1.call-done = bf16[384,4096]{1,0:T(8,128)(2,1)} async-done(((bf16[384,1024]{1,0:T(8,128)(2,1)}), bf16[384,4096]{1,0:T(8,128)(2,1)}) %all-gather.9.cloned.1.call-update) | async-done | bytes 3145744 | tf_op jit(solution)/shard_map/all_gather | solution.py:53
  76.3 2.6 fusion.14
  78.9 52.2 %all-gather.15.cloned.1.call-done = bf16[4096,1024]{1,0:T(8,128)(2,1)} async-done(((bf16[512,1024]{1,0:T(8,128)(2,1)}), bf16[4096,1024]{1,0:T(8,128)(2,1)}) %all-gather.15.cloned.1.call-update) | async-done | bytes 8388624 | tf_op jit(solution)/shard_map/all_gather | solution.py:66
  131.2 7.8 %convolution_convert_fusion = bf16[384,1024]{1,0:T(8,128)(2,1)S(1)} fusion(bf16[4096,1024]{1,0:T(8,128)(2,1)} %all-gather.15.cloned.1.call-done, bf16[384,4096]{1,0:T(8,128)(2,1)} %all-gather.9.cloned.1.call-done, f32[4096]{0:T(1024)S(1)} %convert_element_type.46, f32[384]{0:T(512)S(1)} %add_rsqrt_fusion), kind=kOutput, calls=%fused_computation.45 | convolution fusion | flops 3227910144 | bytes 12338688 | tf_op jit(solution)/shard_map/dot_general | solution.py:62
  139.0 48.4 %all-gather.13.cloned.1.call-done = bf16[4096,1024]{1,0:T(8,128)(2,1)} async-done(((bf16[512,1024]{1,0:T(8,128)(2,1)}), bf16[4096,1024]{1,0:T(8,128)(2,1)}) %all-gather.13.cloned.1.call-update) | async-done | bytes 8388624 | tf_op jit(solution)/shard_map/all_gather | solution.py:65
  187.3 7.8 %convolution_convert_fusion.1 = bf16[384,1024]{1,0:T(8,128)(2,1)S(1)} fusion(bf16[4096,1024]{1,0:T(8,128)(2,1)} %all-gather.13.cloned.1.call-done, bf16[384,4096]{1,0:T(8,128)(2,1)} %all-gather.9.cloned.1.call-done, f32[4096]{0:T(1024)S(1)} %convert_element_type.46, f32[384]{0:T(512)S(1)} %add_rsqrt_fusion), kind=kOutput, calls=%fused_computation.46 | convolution fusion | flops 3227910144 | bytes 12338688 | tf_op jit(solution)/shard_map/dot_general | solution.py:62
  195.1 48.2 %all-gather.11.cloned.1.call-done = bf16[4096,1024]{1,0:T(8,128)(2,1)} async-done(((bf16[512,1024]{1,0:T(8,128)(2,1)}), bf16[4096,1024]{1,0:T(8,128)(2,1)}) %all-gather.11.cloned.1.call-update) | async-done | bytes 8388624 | tf_op jit(solution)/shard_map/all_gather | solution.py:64
  243.4 7.8 %convolution_convert_fusion.2 = bf16[384,1024]{1,0:T(8,128)(2,1)S(1)} fusion(bf16[4096,1024]{1,0:T(8,128)(2,1)} %all-gather.11.cloned.1.call-done, bf16[384,4096]{1,0:T(8,128)(2,1)} %all-gather.9.cloned.1.call-done, f32[4096]{0:T(1024)S(1)} %convert_element_type.46, f32[384]{0:T(512)S(1)} %add_rsqrt_fusion), kind=kOutput, calls=%fused_computation.47 | convolution fusion | flops 3227910144 | bytes 12338688 | tf_op jit(solution)/shard_map/dot_general | solution.py:62
  251.2 2.2 collective-permute-start
  253.5 1.2 copy.44
  254.7 18.6 %gather_fusion = f32[4096,1024]{1,0:T(8,128)} fusion(f32[64,1024]{1,0:T(8,128)S(1)} %bitcast.57, s32[4096]{0:T(1024)S(1)} %broadcast_clamp_fusion), kind=kCustom, calls=%fused_computation | custom fusion | bytes 33570816 | tf_op jit(solution)/shard_map/gather | solution.py:89
  273.3 30.9 %copy.31 = f32[64,64,1024]{1,0,2:T(8,128)} copy(f32[64,64,1024]{2,1,0:T(8,128)} %bitcast.58) | data formatting | bytes 33554432 | tf_op jit(solution)/shard_map/gather | solution.py:89
  304.2 2.1 copy.48
  306.3 0.7 maximum_convert_fusion
  307.0 1.4 fusion.17
  308.4 2.2 copy-done.2
  310.6 0.3 slice_multiply_fusion.3
  310.9 2.7 copy.32
  313.7 16.9 %fusion.24 = f32[6,1024,16]{2,0,1:T(8,128)} fusion(f32[6,64,1024]{1,0,2:T(8,128)} %copy.32, f32[64]{0:T(128)S(1)} %broadcast_subtract_fusion, f32[1024,16]{1,0:T(8,128)S(1)} %copy.30), kind=kOutput, calls=%fused_computation.39 | convolution fusion | flops 76546048 | bytes 2031872 | tf_op jit(solution)/shard_map/sck,bsc->bck/dot_general | solution.py:93
  330.5 2.7 copy.34
  333.2 0.4 while.27
  333.6 10.2 %all-gather.1 = f32[8192,16]{0,1:T(8,128)S(1)} all-gather(f32[1024,16]{0,1:T(8,128)S(1)} %get-tuple-element.128), channel_id=3, replica_groups=mesh['ctx'=8,'dp'=4] {'ctx'}, dimensions={0}, use_global_device_ids=true | all-gather | bytes 589824 | tf_op jit(solution)/shard_map/all_gather | solution.py:17
  343.8 0.3 copy.49
  344.1 9.8 %while.28 = (s32[]{:T(128)}, f32[1024,16]{0,1:T(8,128)S(1)}, s32[]{:T(128)}, f32[8,1024,16]{1,0,2:T(8,128)}, f32[8,1024,16]{1,0,2:T(8,128)S(1)}, /*index=5*/s32[]{:T(128)}, s32[]{:T(128)}) while((s32[]{:T(128)}, f32[1024,16]{0,1:T(8,128)S(1)}, s32[]{:T(128)}, f32[8,1024,16]{1,0,2:T(8,128)}, f32[8,1024,16]{1,0,2:T(8,128)S(1)}, ...), condition=%wide.region_4.5_spmd.clone, body=%wide.region_3.4_spmd.clone.sunk | while | flops 65540 | bytes 524397 | solution.py:29
  344.1 1.1 constant_dynamic-slice_fusion.3
  345.3 1.1 constant_dynamic-slice_fusion.3
  346.5 1.1 constant_dynamic-slice_fusion.3
  347.7 1.1 constant_dynamic-slice_fusion.3
  349.0 1.1 constant_dynamic-slice_fusion.3
  350.2 1.1 constant_dynamic-slice_fusion.3
  351.4 1.1 constant_dynamic-slice_fusion.3
  352.6 1.1 constant_dynamic-slice_fusion.3
  354.0 2.7 copy.38
  356.7 56.2 %fusion.3 = f32[1024,6,64]{2,1,0:T(8,128)S(1)} fusion(f32[6,64,1024]{1,0,2:T(8,128)} %copy.32, f32[64,64,1024]{1,0,2:T(8,128)} %copy.31, pred[64,64]{1,0:T(8,128)(4,1)S(1)} %subtract_compare_fusion), kind=kOutput, calls=%fused_computation.10 | convolution fusion | flops 306184192 | bytes 19927040 | tf_op jit(solution)/shard_map/tsc,bsc->btc/dot_general | solution.py:91
  412.9 12.4 %add_bitcast_fusion = f32[6,64,1024]{1,0,2:T(8,128)} fusion(f32[1024,6,64]{2,1,0:T(8,128)S(1)} %fusion.3, f32[6,1024,16]{2,0,1:T(8,128)S(1)} %copy-done.3, f32[1024,16]{1,0:T(8,128)S(1)} %copy-done.6, f32[64]{0:T(128)S(1)} %broadcast_add_fusion, f32[1024,16]{1,0:T(8,128)S(1)} %copy.30), kind=kOutput, calls=%fused_computation.32 | convolution fusion | flops 77987840 | bytes 3670272 | tf_op jit(solution)/shard_map/tck,bck->btc/dot_general | solution.py:114
  425.3 2.7 copy.39
  428.0 3.9 fusion.29
  432.0 63.6 %all-gather.17.cloned.1.call-done = bf16[384,4096]{1,0:T(8,128)(2,1)} async-done(((bf16[384,1024]{1,0:T(8,128)(2,1)}), bf16[384,4096]{1,0:T(8,128)(2,1)}) %all-gather.17.cloned.1.call-update) | async-done | bytes 3145744 | tf_op jit(solution)/shard_map/all_gather | solution.py:117
  495.5 8.7 %add_convert_fusion = bf16[384,1024]{1,0:T(8,128)(2,1)} fusion(bf16[384,1024]{1,0:T(8,128)(2,1)S(1)} %copy-done.4, bf16[384,4096]{1,0:T(8,128)(2,1)} %all-gather.17.cloned.1.call-done, bf16[4096,1024]{1,0:T(8,128)(2,1)} %all-gather.19.cloned.1.call-done), kind=kOutput, calls=%fused_computation.44 | convolution fusion | flops 3222405120 | bytes 13107200 | tf_op jit(solution)/shard_map/dot_general | solution.py:118
  (76 shorter events, 1.7 us)
Async XLA Ops:
  6.5 1.2 copy-start
  6.5 6.2 %copy-start.10 = (f32[3,3,1024]{2,1,0:T(4,128)S(1)}, f32[3,3,1024]{2,1,0:T(4,128)}, u32[]{:S(2)}) copy-start(f32[3,3,1024]{2,1,0:T(4,128)} %param.21) | copy-start | bytes 110596
  6.5 6.2 %copy-start.8 = (f32[1024,16]{0,1:T(8,128)S(1)}, f32[1024,16]{0,1:T(8,128)}, u32[]{:S(2)}) copy-start(f32[1024,16]{0,1:T(8,128)} %param.22) | copy-start | bytes 196612
  6.5 6.2 %copy-start.9 = (f32[1024,16]{0,1:T(8,128)S(1)}, f32[1024,16]{0,1:T(8,128)}, u32[]{:S(2)}) copy-start(f32[1024,16]{0,1:T(8,128)} %param.23) | copy-start | bytes 196612
  6.5 69.8 %all-gather.9.cloned.1.call-start = ((), (), s32[]{:S(2)}) async-start(), calls=%async_computation | async-start | bytes 3932160 | tf_op jit(solution)/shard_map/all_gather | solution.py:53
  9.9 15.9 %copy-start.12 = (bf16[1024]{0:T(1024)(128)(2,1)S(1)}, bf16[1024]{0:T(1024)(128)(2,1)}, u32[]{:S(2)}) copy-start(bf16[1024]{0:T(1024)(128)(2,1)} %param.17) | copy-start | bytes 6148
  10.0 121.2 %all-gather.15.cloned.1.call-start = ((), (), s32[]{:S(2)}) async-start(), calls=%async_computation.3 | async-start | bytes 9437184 | tf_op jit(solution)/shard_map/all_gather | solution.py:66
  10.7 176.6 %all-gather.13.cloned.1.call-start = ((), (), s32[]{:S(2)}) async-start(), calls=%async_computation.2 | async-start | bytes 9437184 | tf_op jit(solution)/shard_map/all_gather | solution.py:65
  11.5 231.9 %all-gather.11.cloned.1.call-start = ((), (), s32[]{:S(2)}) async-start(), calls=%async_computation.1 | async-start | bytes 9437184 | tf_op jit(solution)/shard_map/all_gather | solution.py:64
  12.0 419.9 %all-gather.19.cloned.1.call-start = ((), (), s32[]{:S(2)}) async-start(), calls=%async_computation.5 | async-start | bytes 9437184 | tf_op jit(solution)/shard_map/all_gather | solution.py:120
  12.6 482.9 %all-gather.17.cloned.1.call-start = ((), (), s32[]{:S(2)}) async-start(), calls=%async_computation.4 | async-start | bytes 3932160 | tf_op jit(solution)/shard_map/all_gather | solution.py:117
  13.0 65.9 %copy-start.5 = (f32[1024,16]{1,0:T(8,128)}, f32[1024,16]{1,0:T(8,128)S(1)}, u32[]{:S(2)}) copy-start(f32[1024,16]{1,0:T(8,128)S(1)} %copy.47) | copy-start | bytes 196612
  251.2 55.1 %collective-permute-start = (bf16[2,3072]{1,0:T(2,128)(2,1)S(1)}, bf16[2,3072]{1,0:T(2,128)(2,1)S(1)}, u32[]{:S(2)}, u32[]{:S(2)}) collective-permute-start(bf16[2,3072]{1,0:T(2,128)(2,1)S(1)} %pad_maximum_fusion), channel_id=1, source_target_pairs={{0,4},{4,8},{8,12},{12,16},{16,20},{20,24},{24,28},{1,5},{5,9},{9,... | collective-permute-start | bytes 36872 | tf_op jit(solution)/shard_map/ppermute | solution.py:12
  308.4 2.2 copy-start.2
  313.7 19.5 %copy-start.7 = (f32[6,1024,16]{1,2,0:T(8,128)S(1)}, f32[6,1024,16]{1,2,0:T(8,128)}, u32[]{:S(2)}) copy-start(f32[6,1024,16]{1,2,0:T(8,128)} %custom-call.4) | copy-start | bytes 1179652
  356.7 56.2 %copy-start.3 = (f32[6,1024,16]{2,0,1:T(8,128)S(1)}, f32[6,1024,16]{2,0,1:T(8,128)}, u32[]{:S(2)}) copy-start(f32[6,1024,16]{2,0,1:T(8,128)} %copy.38) | copy-start | bytes 1179652
  356.7 56.2 %copy-start.6 = (f32[1024,16]{1,0:T(8,128)S(1)}, f32[1024,16]{1,0:T(8,128)}, u32[]{:S(2)}) copy-start(f32[1024,16]{1,0:T(8,128)} %copy-done.5) | copy-start | bytes 196612
  425.3 2.7 copy-start.11
  428.0 67.6 %copy-start.4 = (bf16[384,1024]{1,0:T(8,128)(2,1)S(1)}, bf16[384,1024]{1,0:T(8,128)(2,1)}, u32[]{:S(2)}) copy-start(bf16[384,1024]{1,0:T(8,128)(2,1)} %convolution_convert_fusion.3) | copy-start | bytes 2359300
  495.5 8.7 %copy-start.1 = (bf16[512,1024]{1,0:T(8,128)(2,1)S(1)}, bf16[512,1024]{1,0:T(8,128)(2,1)}, u32[]{:S(2)}) copy-start(bf16[512,1024]{1,0:T(8,128)(2,1)} %param.16) | copy-start | bytes 3145732
Sparse Core Ops, SparseCore 0:
  10.1 66.2 all-gather.8
  78.2 52.8 all-gather.14
  133.1 54.2 all-gather.12
  189.1 54.2 all-gather.10
  245.1 54.2 all-gather.18
  432.1 63.4 all-gather.16
where the time goes:
time: 521 us; the launch traced here: 512 us
  waiting for transfers between devices  240 us (46%)
  matrix products  120 us (23%)
  local copies, waits for them, and re-layouts  77.1 us (15%)
  blocking collectives  35.9 us (7%)
  other arithmetic  22.2 us (4%)
  between operations  14.2 us (3%)
    all_gather x1, waiting for transfers between devices, shards(): all_mixed = lax.all_gather(mixed, 'dp', axis=1, tiled=True)  63.6 us
    dot_general x1, matrix products, shards(): inside = jnp.einsum('tsc,bsc->btc', toeplitz, pieces, precision=highest)  56.2 us
    all_gather x1, waiting for transfers between devices, shards(): value_proj = add_rows(lax.all_gather(w_value, 'ctx', axis=0, tiled=True))  52.2 us
    gather x2, local copies, waits for them, and re-layouts, shards(): kernel[jnp.maximum(offsets, 0)]  49.5 us
    all_gather x1, waiting for transfers between devices, shards(): key_proj = add_rows(lax.all_gather(w_key, 'ctx', axis=0, tiled=True))  48.4 us
    all_gather x1, waiting for transfers between devices, shards(): query_proj = add_rows(lax.all_gather(w_query, 'ctx', axis=0, tiled=True))  48.2 us
    all_gather x1, waiting for transfers between devices, shards(): lax.all_gather(embedded, 'dp', axis=1, tiled=True)  24.7 us
    dot_general x3, matrix products, add_rows(): return jnp.dot(normed, piece, preferred_element_type=jnp.float32)  23.4 us
  transfers between devices with their start and end apart: 7, of which 5 were waited for; matrix products, arithmetic and copies ran while one was open for 40% of the time, Pallas kernels for 0%

commit v1 on v0

--- a/solution.py
+++ b/solution.py
@@ -3,7 +3,15 @@
 import jax
 import jax.numpy as jnp
 from jax import lax
+
+from jax.experimental import pallas as pl
+from jax.experimental.pallas import tpu as pltpu
 from jax.sharding import PartitionSpec as P
+
+MESH = pl.DeviceIdType.MESH
+LANES = 128
+SUBLANES = 8
+VMEM_BYTES = 56 << 20
 
 
 def shifted(value, axis, steps):
@@ -123,6 +131,614 @@
     return (embedded.astype(jnp.float32) + output).astype(jnp.bfloat16)
 
 
+def remote(src, dst, send, recv, **where):
+    return pltpu.make_async_remote_copy(
+        src_ref=src,
+        dst_ref=dst,
+        send_sem=send,
+        recv_sem=recv,
+        device_id=where,
+        device_id_type=MESH,
+    )
+
+
+def greet(ctx_peers, dp_peers):
+    barrier = pltpu.get_barrier_semaphore()
+    for peer in ctx_peers:
+        pl.semaphore_signal(barrier, inc=1, device_id={"ctx": peer}, device_id_type=MESH)
+    for peer in dp_peers:
+        pl.semaphore_signal(barrier, inc=1, device_id={"dp": peer}, device_id_type=MESH)
+    pl.semaphore_wait(barrier, len(ctx_peers) + len(dp_peers))
+
+
+def flip(index, bit):
+    return index + bit - 2 * bit * (lax.rem(index // bit, 2))
+
+
+def spread_kernel(
+    n_ctx,
+    n_dp,
+    ids_ref,
+    gain_ref,
+    table_ref,
+    wq_ref,
+    wk_ref,
+    wv_ref,
+    ids_out,
+    gain_out,
+    table_out,
+    w_out,
+    own_w,
+    own_table,
+    w_send,
+    w_recv,
+    id_send,
+    id_recv,
+    gain_send,
+    gain_recv,
+    z_send,
+    z_recv,
+    core_send,
+    core_recv,
+    local,
+):
+    me, at = lax.axis_index("ctx"), lax.axis_index("dp")
+    depth, wide = wq_ref.shape[0], wq_ref.shape[1] // n_ctx
+    vocab = table_ref.shape[0]
+    chunks = z_send.shape[2]
+    part = vocab // 2 // chunks
+    partner = flip(me, 1)
+    ctx_peers = [lax.rem(me + d, n_ctx) for d in range(1, n_ctx)]
+    dp_peers = [lax.rem(at + d, n_dp) for d in range(1, n_dp)]
+    greet(ctx_peers, dp_peers)
+    rows = pl.ds(pl.multiple_of(me * depth, depth), depth)
+    weights = (wq_ref, wk_ref, wv_ref)
+
+    def half_chunk(core, k):
+        return pl.ds(pl.multiple_of((core * chunks + k) * part, part), part)
+
+    def z_copy(source, k, way, hop, peer):
+        piece = half_chunk(lax.rem(me, 2), k)
+        src = table_ref.at[piece] if hop == 0 else table_out.at[source, piece]
+        return remote(
+            src,
+            table_out.at[source, piece],
+            z_send.at[way, hop, k],
+            z_recv.at[source, k],
+            dp=peer,
+        )
+
+    def core_copy(source, core, k):
+        piece = half_chunk(core, k)
+        return remote(
+            table_out.at[source, piece],
+            table_out.at[source, piece],
+            core_send.at[source, k],
+            core_recv.at[source, k],
+            ctx=partner,
+        )
+
+    for k in range(chunks):
+
+        @pl.when(at < n_dp - 1)
+        def _():
+            z_copy(at, k, 0, 0, at + 1).start()
+
+        @pl.when(at > 0)
+        def _():
+            z_copy(at, k, 1, 0, at - 1).start()
+
+    sends = []
+    for d, peer in enumerate(ctx_peers):
+        copy = remote(ids_ref, ids_out.at[me], id_send.at[d], id_recv.at[me], ctx=peer)
+        copy.start()
+        sends.append(copy)
+    for d, peer in enumerate(dp_peers):
+        copy = remote(gain_ref, gain_out.at[at], gain_send.at[d], gain_recv.at[at], dp=peer)
+        copy.start()
+        sends.append(copy)
+    for d, peer in enumerate(ctx_peers):
+        for w, weight in enumerate(weights):
+            copy = remote(
+                weight.at[:, pl.ds(pl.multiple_of(peer * wide, wide), wide)],
+                w_out.at[rows, pl.ds(w * wide, wide)],
+                w_send.at[d, w],
+                w_recv.at[me, w],
+                ctx=peer,
+            )
+            copy.start()
+            sends.append(copy)
+    into = [
+        pltpu.make_async_copy(
+            weight.at[:, pl.ds(pl.multiple_of(me * wide, wide), wide)],
+            own_w.at[:, pl.ds(w * wide, wide)],
+            local.at[w],
+        )
+        for w, weight in enumerate(weights)
+    ]
+    into.append(pltpu.make_async_copy(table_ref, own_table, local.at[3]))
+    into.append(pltpu.make_async_copy(ids_ref, ids_out.at[me], local.at[4]))
+    into.append(pltpu.make_async_copy(gain_ref, gain_out.at[at], local.at[5]))
+    for copy in into:
+        copy.start()
+    for copy in into:
+        copy.wait()
+    out = [
+        pltpu.make_async_copy(own_w, w_out.at[rows], local.at[0]),
+        pltpu.make_async_copy(own_table, table_out.at[at], local.at[1]),
+    ]
+    for copy in out:
+        copy.start()
+
+    core = lax.rem(me, 2)
+    for hop in range(1, n_dp):
+        for k in range(chunks):
+
+            @pl.when(at - hop >= 0)
+            def _():
+                z_copy(at - hop, k, 0, 0, at).wait_recv()
+                core_copy(at - hop, core, k).start()
+
+                if hop < n_dp - 1:
+
+                    @pl.when(at < n_dp - 1)
+                    def _():
+                        z_copy(at - hop, k, 0, hop, at + 1).start()
+
+            @pl.when(at + hop <= n_dp - 1)
+            def _():
+                z_copy(at + hop, k, 1, 0, at).wait_recv()
+                core_copy(at + hop, core, k).start()
+
+                if hop < n_dp - 1:
+
+                    @pl.when(at > 0)
+                    def _():
+                        z_copy(at + hop, k, 1, hop, at - 1).start()
+
+    for d in range(1, n_dp):
+        source = lax.rem(at + d, n_dp)
+        for k in range(chunks):
+            core_copy(source, 1 - core, k).wait_recv()
+            core_copy(source, core, k).wait_send()
+    for hop in range(n_dp - 1):
+        for k in range(chunks):
+
+            @pl.when((at - hop >= 0) & (at < n_dp - 1))
+            def _():
+                z_copy(at - hop, k, 0, hop, at + 1).wait_send()
+
+            @pl.when((at + hop <= n_dp - 1) & (at > 0))
+            def _():
+                z_copy(at + hop, k, 1, hop, at - 1).wait_send()
+
+    for d, peer in enumerate(ctx_peers):
+        remote(ids_ref, ids_out.at[peer], id_send.at[d], id_recv.at[peer], ctx=peer).wait_recv()
+        theirs = pl.ds(pl.multiple_of(peer * depth, depth), depth)
+        for w, weight in enumerate(weights):
+            remote(
+                weight.at[:, pl.ds(pl.multiple_of(peer * wide, wide), wide)],
+                w_out.at[theirs, pl.ds(w * wide, wide)],
+                w_send.at[d, w],
+                w_recv.at[peer, w],
+                ctx=peer,
+            ).wait_recv()
+    for d, peer in enumerate(dp_peers):
+        remote(gain_ref, gain_out.at[peer], gain_send.at[d], gain_recv.at[peer], dp=peer).wait_recv()
+    for copy in sends:
+        copy.wait_send()
+    for copy in out:
+        copy.wait()
+
+
+def spread(n_ctx, n_dp, ids, gain, table, w_query, w_key, w_value):
+    depth, wide = w_query.shape[0], w_query.shape[1] // n_ctx
+    chunks = 2
+    anywhere = pl.BlockSpec(memory_space=pl.ANY)
+    dma = pltpu.SemaphoreType.DMA
+    return pl.pallas_call(
+        lambda *refs: spread_kernel(n_ctx, n_dp, *refs),
+        name="spread",
+        out_shape=(
+            jax.ShapeDtypeStruct((n_ctx, *ids.shape), ids.dtype),
+            jax.ShapeDtypeStruct((n_dp, *gain.shape), gain.dtype),
+            jax.ShapeDtypeStruct((n_dp, *table.shape), table.dtype),
+            jax.ShapeDtypeStruct((n_ctx * depth, 3 * wide), w_query.dtype),
+        ),
+        in_specs=[anywhere] * 6,
+        out_specs=[anywhere] * 4,
+        scratch_shapes=[
+            pltpu.VMEM((depth, 3 * wide), w_query.dtype),
+            pltpu.VMEM(table.shape, table.dtype),
+            dma((n_ctx - 1, 3)),
+            dma((n_ctx, 3)),
+            dma((n_ctx - 1,)),
+            dma((n_ctx,)),
+            dma((n_dp - 1,)),
+            dma((n_dp,)),
+            dma((2, n_dp - 1, chunks)),
+            dma((n_dp, chunks)),
+            dma((n_dp, chunks)),
+            dma((n_dp, chunks)),
+            dma((6,)),
+        ],
+        compiler_params=pltpu.CompilerParams(
+            collective_id=0, has_side_effects=True, vmem_limit_bytes=8 << 20
+        ),
+    )(ids, gain, table, w_query, w_key, w_value)
+
+
+def mix_kernel(
+    ids_ref,
+    gain_ref,
+    table_ref,
+    w_ref,
+    filt_ref,
+    rate_ref,
+    residue_ref,
+    skip_ref,
+    out_ref,
+    proj,
+    gated,
+    query,
+):
+    n_dp, vocab, width = table_ref.shape
+    features = n_dp * width
+    taps = filt_ref.shape[0]
+    modes = rate_ref.shape[0]
+    segments, steps, lanes = out_ref.shape
+    lead = proj.shape[0] - segments * steps
+    total = jnp.zeros((vocab, 1), jnp.float32)
+    for b in range(n_dp):
+        block = table_ref[b].astype(jnp.float32)
+        total = total + jnp.sum(block * block, axis=1, keepdims=True)
+    scale = lax.rsqrt(total / features + 1e-06)
+    rows = jnp.zeros((vocab, 3 * lanes), jnp.float32)
+    for b in range(n_dp):
+        block = table_ref[b].astype(jnp.float32)
+        normed = (block * scale * gain_ref[:, b * width : (b + 1) * width]).astype(jnp.bfloat16)
+        rows = rows + jnp.dot(
+            normed, w_ref[b * width : (b + 1) * width, :], preferred_element_type=jnp.float32
+        )
+    rows = rows.astype(jnp.bfloat16)
+    size = lead
+
+    def place(n, carry):
+        here = pl.ds(pl.multiple_of(n * size, size), size)
+        names = lax.broadcasted_iota(jnp.int32, (size, vocab), 1)
+        one_hot = (ids_ref[here, :] == names).astype(jnp.float32).astype(jnp.bfloat16)
+        proj[here, :] = jnp.dot(one_hot, rows, preferred_element_type=jnp.float32)
+        return carry
+
+    lax.fori_loop(0, proj.shape[0] // size, place, 0)
+
+    def convolve(n, carry):
+        start = n * size + lead
+        conv = [jnp.zeros((size, lanes), jnp.float32) for _ in range(3)]
+        for tap in range(taps):
+            here = pl.ds(pl.multiple_of(start - tap * segments, segments), size)
+            piece = proj[here, :]
+            for w in range(3):
+                conv[w] = conv[w] + filt_ref[tap, w : w + 1, :] * piece[:, w * lanes : (w + 1) * lanes]
+        there = pl.ds(pl.multiple_of(n * size, size), size)
+        query[there, :] = conv[0]
+        gated[there, :] = conv[1] * conv[2]
+        return carry
+
+    lax.fori_loop(0, segments * steps // size, convolve, 0)
+
+    def spread_rows(row):
+        return jnp.broadcast_to(row, (segments, lanes))
+
+    decay = [spread_rows(jnp.exp(-rate_ref[m : m + 1, :])) for m in range(modes)]
+    unroll = 4
+
+    def ends(n, state):
+        for u in range(unroll):
+            row = gated[pl.ds(pl.multiple_of((n * unroll + u) * segments, segments), segments), :]
+            state = tuple(d * s + row for d, s in zip(decay, state))
+        return state
+
+    zero = jnp.zeros((segments, lanes), jnp.float32)
+    state = lax.fori_loop(0, steps // unroll, ends, (zero,) * modes)
+    place_of = lax.broadcasted_iota(jnp.int32, (segments, lanes), 0)
+
+    def later(value, by):
+        return jnp.where(place_of >= by, pltpu.roll(value, by, 0), 0.0)
+
+    entering = []
+    for m in range(modes):
+        value = later(state[m], 1)
+        by = 1
+        while by < segments:
+            jump = jnp.exp(-rate_ref[m : m + 1, :] * float(steps * by))
+            value = value + jump * later(value, by)
+            by *= 2
+        entering.append(value)
+    strength = [
+        spread_rows(residue_ref[m : m + 1, :] * jnp.sqrt(2.0 * rate_ref[m : m + 1, :]))
+        for m in range(modes)
+    ]
+    skip = spread_rows(skip_ref[...])
+
+    def advance(n, state):
+        for u in range(unroll):
+            here = pl.ds(pl.multiple_of((n * unroll + u) * segments, segments), segments)
+            row = gated[here, :]
+            state = tuple(d * s + row for d, s in zip(decay, state))
+            terms = [c * s for c, s in zip(strength, state)]
+            while len(terms) > 1:
+                terms = [a + b for a, b in zip(terms[::2], terms[1::2])] + (
+                    [terms[-1]] if len(terms) % 2 else []
+                )
+            query[here, :] = query[here, :] * (terms[0] + skip * row)
+        return state
+
+    lax.fori_loop(0, steps // unroll, advance, tuple(entering))
+    for s in range(segments):
+        out_ref[s] = query[pl.ds(s, steps, stride=segments), :].astype(jnp.bfloat16)
+
+
+def mix(ids, gain, table, w, filt, rate, residue, skip, segments, steps):
+    whole = pl.BlockSpec(memory_space=pltpu.VMEM)
+    wide = w.shape[1]
+    lanes = wide // 3
+    return pl.pallas_call(
+        mix_kernel,
+        name="mix",
+        out_shape=jax.ShapeDtypeStruct((segments, steps, lanes), jnp.bfloat16),
+        in_specs=[whole] * 8,
+        out_specs=whole,
+        scratch_shapes=[
+            pltpu.VMEM((ids.shape[0], wide), jnp.float32),
+            pltpu.VMEM((segments * steps, lanes), jnp.float32),
+            pltpu.VMEM((segments * steps, lanes), jnp.float32),
+        ],
+        compiler_params=pltpu.CompilerParams(vmem_limit_bytes=VMEM_BYTES),
+    )(ids, gain, table, w, filt, rate, residue, skip)
+
+
+def collect_kernel(
+    n_ctx,
+    n_dp,
+    mixed_ref,
+    weight_ref,
+    mixed_out,
+    weight_out,
+    own_mixed,
+    own_weight,
+    a_send,
+    slot_recv,
+    z_send,
+    w_send,
+    w_recv,
+    core_send,
+    core_recv,
+    local,
+):
+    me, at = lax.axis_index("ctx"), lax.axis_index("dp")
+    depth, lanes = weight_ref.shape[0], mixed_ref.shape[2]
+    bits = [1 << b for b in range(n_ctx.bit_length() - 1)]
+    ctx_peers = [lax.rem(me + d, n_ctx) for d in range(1, n_ctx)]
+    near = [(at - 1, at > 0), (at + 1, at < n_dp - 1)]
+    barrier = pltpu.get_barrier_semaphore()
+    dp_peers = [lax.rem(at + d, n_dp) for d in range(1, n_dp)]
+    greet(ctx_peers, dp_peers)
+    partner, side, up = flip(me, 1), flip(me, 2), flip(me, 4)
+    across = flip(side, 4)
+    half = depth // 2
+
+    def slot(source, k):
+        start = (source * n_ctx + k) * lanes
+        return mixed_out.at[:, pl.ds(pl.multiple_of(start, lanes), lanes)]
+
+    def turn(d, peer):
+        return remote(mixed_ref.at[peer], slot(at, me), a_send.at[d - 1], slot_recv.at[at, me], ctx=peer)
+
+    def block(owner, first=0, count=None):
+        count = depth if count is None else count
+        start = pl.multiple_of(owner * depth + first, half)
+        return weight_out.at[pl.ds(start, count)]
+
+    for d, peer in enumerate(ctx_peers):
+        turn(d + 1, peer).start()
+    into = [
+        pltpu.make_async_copy(mixed_ref.at[me], own_mixed, local.at[0]),
+        pltpu.make_async_copy(weight_ref, own_weight, local.at[1]),
+    ]
+    for copy in into:
+        copy.start()
+
+    def z_copy(source, d, way, hop, peer):
+        k = lax.rem(me + d, n_ctx)
+        src = mixed_ref.at[me] if hop == 0 and d == 0 else slot(source, k)
+        return remote(src, slot(source, k), z_send.at[way, hop, d], slot_recv.at[source, k], dp=peer)
+
+    def recv(source, d):
+        k = lax.rem(me + d, n_ctx)
+        z_copy_like = remote(slot(source, k), slot(source, k), z_send.at[0, 0, d], slot_recv.at[source, k], ctx=partner)
+        z_copy_like.wait_recv()
+
+    def first_hop(d):
+        @pl.when(at < n_dp - 1)
+        def _():
+            z_copy(at, d, 0, 0, at + 1).start()
+
+        @pl.when(at > 0)
+        def _():
+            z_copy(at, d, 1, 0, at - 1).start()
+
+    first_hop(0)
+    own = [
+        remote(weight_ref, block(me), w_send.at[0], w_recv.at[0], ctx=side),
+        remote(weight_ref, block(me), w_send.at[1], w_recv.at[1], ctx=up),
+        remote(weight_ref, block(me), w_send.at[2], w_recv.at[2], ctx=partner),
+    ]
+    for copy in own:
+        copy.start()
+    for copy in into:
+        copy.wait()
+    out = [
+        pltpu.make_async_copy(own_mixed, slot(at, me), local.at[0]),
+        pltpu.make_async_copy(own_weight, block(me), local.at[1]),
+    ]
+    for copy in out:
+        copy.start()
+    for d in range(1, n_ctx):
+        recv(at, d)
+        first_hop(d)
+
+    for hop in range(1, n_dp):
+        for d in range(n_ctx):
+
+            @pl.when(at - hop >= 0)
+            def _():
+                recv(at - hop, d)
+
+                if hop < n_dp - 1:
+
+                    @pl.when(at < n_dp - 1)
+                    def _():
+                        z_copy(at - hop, d, 0, hop, at + 1).start()
+
+            @pl.when(at + hop <= n_dp - 1)
+            def _():
+                recv(at + hop, d)
+
+                if hop < n_dp - 1:
+
+                    @pl.when(at > 0)
+                    def _():
+                        z_copy(at + hop, d, 1, hop, at - 1).start()
+
+        if hop == 1:
+            own[0].wait_recv()
+            own[1].wait_recv()
+            passed = [
+                remote(block(side, 0, half), block(side, 0, half), w_send.at[3], w_recv.at[3], ctx=up),
+                remote(block(up, half, half), block(up, half, half), w_send.at[4], w_recv.at[4], ctx=side),
+                remote(block(side), block(side), core_send.at[0], core_recv.at[0], ctx=partner),
+                remote(block(up), block(up), core_send.at[1], core_recv.at[1], ctx=partner),
+            ]
+            for copy in passed:
+                copy.start()
+    passed[0].wait_recv()
+    passed[1].wait_recv()
+    last = [
+        remote(block(across, 0, half), block(across, 0, half), core_send.at[2], core_recv.at[2], ctx=partner),
+        remote(block(across, half, half), block(across, half, half), core_send.at[3], core_recv.at[3], ctx=partner),
+    ]
+    for copy in last:
+        copy.start()
+    own[2].wait_recv()
+    passed[2].wait_recv()
+    passed[3].wait_recv()
+    for copy in last:
+        copy.wait_recv()
+    for copy in own + passed + last:
+        copy.wait_send()
+    for d, peer in enumerate(ctx_peers):
+        turn(d + 1, peer).wait_send()
+    for hop in range(n_dp - 1):
+        for d in range(n_ctx):
+
+            @pl.when((at - hop >= 0) & (at < n_dp - 1))
+            def _():
+                z_copy(at - hop, d, 0, hop, at + 1).wait_send()
+
+            @pl.when((at + hop <= n_dp - 1) & (at > 0))
+            def _():
+                z_copy(at + hop, d, 1, hop, at - 1).wait_send()
+
+    for copy in out:
+        copy.wait()
+
+
+def collect(n_ctx, n_dp, mixed, weight):
+    depth, columns = weight.shape
+    steps, lanes = mixed.shape[1:]
+    anywhere = pl.BlockSpec(memory_space=pl.ANY)
+    dma = pltpu.SemaphoreType.DMA
+    return pl.pallas_call(
+        lambda *refs: collect_kernel(n_ctx, n_dp, *refs),
+        name="collect",
+        out_shape=(
+            jax.ShapeDtypeStruct((steps, n_dp * n_ctx * lanes), mixed.dtype),
+            jax.ShapeDtypeStruct((n_ctx * depth, columns), weight.dtype),
+        ),
+        in_specs=[anywhere] * 2,
+        out_specs=[anywhere] * 2,
+        scratch_shapes=[
+            pltpu.VMEM((steps, lanes), mixed.dtype),
+            pltpu.VMEM((depth, columns), weight.dtype),
+            dma((n_ctx - 1,)),
+            dma((n_dp, n_ctx)),
+            dma((2, n_dp - 1, n_ctx)),
+            dma((5,)),
+            dma((5,)),
+            dma((4,)),
+            dma((4,)),
+            dma((2,)),
+        ],
+        compiler_params=pltpu.CompilerParams(
+            collective_id=1, has_side_effects=True, vmem_limit_bytes=8 << 20
+        ),
+    )(mixed, weight)
+
+
+def by_channel(
+    n_ctx,
+    n_dp,
+    ids,
+    embed_table,
+    norm_gain,
+    w_query,
+    w_key,
+    w_value,
+    short_filter,
+    pole_rate,
+    residue,
+    skip_gain,
+    w_out,
+):
+    vocab = embed_table.shape[0]
+    tok_rows = ids.shape[0]
+    taps = short_filter.shape[0]
+    me = lax.axis_index("ctx")
+    gain = norm_gain.astype(jnp.float32).reshape(-1, LANES)
+    all_ids, all_gain, all_table, w_mine = spread(
+        n_ctx, n_dp, ids.reshape(-1, LANES), gain, embed_table, w_query, w_key, w_value
+    )
+    all_gain = all_gain.reshape(1, -1)
+    by_step = all_ids.reshape(n_ctx, tok_rows)
+    before = jnp.concatenate(
+        [jnp.full((1, taps - 1), -1, jnp.int32), by_step[:-1, tok_rows - (taps - 1) :]], axis=0
+    )
+    pad = jnp.full((LANES - n_ctx * (taps - 1),), -1, jnp.int32)
+    ordered = jnp.concatenate([pad, before.T.reshape(-1), by_step.T.reshape(-1)])[:, None]
+
+    def mine(value, axis):
+        return lax.dynamic_slice_in_dim(value, me * LANES, LANES, axis)
+
+    mixed = mix(
+        ordered,
+        all_gain,
+        all_table,
+        w_mine,
+        mine(short_filter, 2),
+        mine(pole_rate, 0).T,
+        mine(residue, 0).T,
+        mine(skip_gain, 0)[None, :],
+        n_ctx,
+        tok_rows,
+    )
+    all_mixed, all_rows = collect(n_ctx, n_dp, mixed, w_out)
+    one_hot = (ids[:, None] == jnp.arange(vocab, dtype=jnp.int32)[None, :]).astype(jnp.bfloat16)
+    embedded = jnp.dot(one_hot, embed_table, preferred_element_type=jnp.float32)
+    output = jnp.dot(all_mixed, all_rows, preferred_element_type=jnp.float32)
+    return (embedded + output).astype(jnp.bfloat16)
+
+
 def solution(mesh):
     placed = (
         P("ctx"),
@@ -137,6 +753,20 @@
         P("dp"),
         P("ctx", "dp"),
     )
+    n_ctx, n_dp = mesh.shape["ctx"], mesh.shape["dp"]
+
+    def body(*args):
+        ids, w_query = args[0], args[3]
+        fits = (
+            n_ctx == SUBLANES
+            and n_dp > 1
+            and w_query.shape[1] == n_ctx * LANES
+            and ids.shape[0] % LANES == 0
+        )
+        if fits:
+            return by_channel(n_ctx, n_dp, *args)
+        return shards(*args)
+
     return jax.shard_map(
-        shards, mesh=mesh, in_specs=placed, out_specs=P("ctx", "dp"), check_vma=False
-    )
+        body, mesh=mesh, in_specs=placed, out_specs=P("ctx", "dp"), check_vma=False
+    )

time: 521 us -> 152 us (0.29); the launches traced: 512 us -> 152 us
  waiting for transfers between devices: 240 us -> 0 us
  Pallas kernels: 0 us -> 129 us
  matrix products: 120 us -> 5.05 us
  local copies, waits for them, and re-layouts: 77.1 us -> 17.1 us
  blocking collectives: 35.9 us -> 0 us
  other arithmetic: 22.2 us -> 0.68 us
  between operations: 14.2 us -> 0.1 us
    all_gather x6 -> x0, waiting for transfers between devices: 237 us -> none  [the longest x1 63.6 us: shards(): all_mixed = lax.all_gather(mixed, 'dp', axis=1, tiled=True)]
    pallas_call x0 -> x3, Pallas kernels: none -> 129 us  [the longest x1 63.5 us: collect(): pl.pallas_call(lambda *refs: collect_kernel(n_ctx, n_dp, *refs), name='co...]
    dot_general x8 -> x2, matrix products: 120 us -> 5.05 us  [the longest x1 3.52 us: by_channel(): output = jnp.dot(all_mixed, all_rows, preferred_element_type=jnp.float32)]
    gather x2 -> x0, local copies, waits for them, and re-layouts: 49.5 us -> none  [shards(): kernel[jnp.maximum(offsets, 0)]]
    all_gather x3 -> x0, blocking collectives: 35.9 us -> none  [the longest x2 21 us: entering_2(): everything = jax.tree.map(lambda part: lax.all_gather(part, axis), value)]
    unnamed x3 -> x0, other arithmetic: 12.6 us -> none
    dynamic_slice x8 -> x1, local copies, waits for them, and re-layouts: 9.15 us -> 0.59 us  [mine(): return lax.dynamic_slice_in_dim(value, me * LANES, LANES, axis)]
    add x2 -> x0, local copies, waits for them, and re-layouts: 5.42 us -> none  [the longest x1 2.71 us: shards(): entering + jnp.exp(-pole_rate[None] * block_pos[:, None, None]) * incomin...]
  transfers between devices with their start and end apart: 7 -> 0, of which waited for: 5 -> 0; matrix products, arithmetic and copies ran while one was open for 40% -> 0% of each run, Pallas kernels for 0% -> 0%
where the time goes in v1:
time: 152 us
  Pallas kernels  129 us (85%)
  local copies, waits for them, and re-layouts  17.1 us (11%)
  matrix products  5.05 us (3%)
    pallas_call x1, Pallas kernels, collect(): pl.pallas_call(lambda *refs: collect_kernel(n_ctx, n_dp, *refs), name='co...  63.5 us
    pallas_call x1, Pallas kernels, spread(): pl.pallas_call(lambda *refs: spread_kernel(n_ctx, n_dp, *refs), name='spr...  42.7 us
    pallas_call x1, Pallas kernels, mix(): pl.pallas_call(mix_kernel, name='mix', out_shape=jax.ShapeDtypeStruct((se...  22.5 us
    unnamed x28, local copies, waits for them, and re-layouts  11 us
    dot_general x1, matrix products, by_channel(): output = jnp.dot(all_mixed, all_rows, preferred_element_type=jnp.float32)  3.52 us

profile of v1, /device:TPU:0, one launch (start us, length us, event | category | flops | bytes accessed | tf_op | source)
XLA Modules:
  0.0 151.6 jit_solution(11608993947536309430)
XLA Ops:
  0.0 0.0 copy-start
  0.0 1.3 dynamic-slice_bitcast_fusion.2.skip_ref
  1.3 0.7 bitcast_convert_fusion.refs_1_
  2.0 0.0 copy-done
  2.0 0.6 constant_dynamic-slice_fusion.filt_ref
  2.6 1.3 dynamic-slice_bitcast_fusion
  3.9 0.0 copy-start.1
  3.9 1.2 copy-done.1
  5.2 0.0 copy-start.6
  5.2 1.2 copy-done.6
  6.4 0.0 copy-start.7
  6.4 1.2 copy-done.7
  7.6 0.0 copy-start.8
  7.6 1.2 copy-done.8
  8.8 0.0 copy-start.11
  8.8 0.7 copy-done.11
  9.5 42.7 %spread.1 = (s32[8,3,128]{2,1,0:T(4,128)S(1)}, f32[4,8,128]{2,1,0:T(8,128)S(1)}, bf16[4,512,1024]{2,1,0:T(8,128)(2,1)S(1)}, bf16[4096,384]{1,0:T(8,128)(2,1)S(1)}) custom-call(s32[3,128]{1,0:T(4,128)S(1)} %bitcast.29, f32[8,128]{1,0:T(8,128)S(1)} %bitcast_convert_fusion.refs_1_, bf16[512,1024]{1,0:T(8,128)(2,1)S(1)} %copy-done.1, ...), custom_call_target="tpu_custom_call" | custom-call | tf_op jit(solution)/shard_map/spread/pallas_call | solution.py:339
  52.2 0.0 copy-start.3
  52.2 1.9 %copy-done.3 = bf16[4,512,1024]{2,1,0:T(8,128)(2,1)} copy-done((bf16[4,512,1024]{2,1,0:T(8,128)(2,1)}, bf16[4,512,1024]{2,1,0:T(8,128)(2,1)S(1)}, u32[]{:S(2)}) %copy-start.3) | copy-done | bytes 4194328
  54.2 0.0 copy-start.4
  54.2 1.7 %copy-done.4 = bf16[4096,384]{1,0:T(8,128)(2,1)} copy-done((bf16[4096,384]{1,0:T(8,128)(2,1)}, bf16[4096,384]{1,0:T(8,128)(2,1)S(1)}, u32[]{:S(2)}) %copy-start.4) | copy-done | bytes 3145752
  55.9 0.0 copy-start.10
  55.9 0.6 copy-done.10
  56.5 0.1 slice.4
  56.5 0.1 copy.13
  56.6 0.1 reshape.25
  56.7 0.1 copy.14
  56.8 0.1 reshape.26
  57.0 0.1 concatenate.7
  57.1 2.3 %broadcast_in_dim.14.ids_ref = s32[3200,1]{1,0:T(8,128)} reshape(s32[3200]{0:T(1024)S(1)} %concatenate.7) | data formatting | bytes 25600 | tf_op jit(solution)/shard_map/broadcast_in_dim | solution.py:718
  59.4 0.0 copy-start.9
  59.4 22.5 %mix.1.refs_0_ = bf16[8,384,128]{2,1,0:T(8,128)(2,1)} custom-call(s32[3200,1]{1,0:T(8,128)} %broadcast_in_dim.14.ids_ref, f32[1,4096]{1,0:T(1,128)} %bitcast.28, bf16[4,512,1024]{2,1,0:T(8,128)(2,1)} %copy-done.3, bf16[4096,384]{1,0:T(8,128)(2,1)} %copy-done.4, f32[3,3,128]{2,1,0:T(4,128)} %constant_dynamic-slice_fusion.filt_ref, ...), custom_call_target="tpu_custom_call" | custom-call | tf_op jit(solution)/shard_map/mix/pallas_call | solution.py:486
  81.9 0.0 copy-done.9
  81.9 0.0 copy-start.5
  81.9 1.1 copy-done.5
  83.0 63.5 %collect.1 = (bf16[384,4096]{1,0:T(8,128)(2,1)S(1)}, bf16[4096,1024]{1,0:T(8,128)(2,1)S(1)}) custom-call(bf16[8,384,128]{2,1,0:T(8,128)(2,1)S(1)} %copy-done.5, bf16[512,1024]{1,0:T(8,128)(2,1)S(1)} %copy-done.9), custom_call_target="tpu_custom_call" | custom-call | tf_op jit(solution)/shard_map/collect/pallas_call | solution.py:662
  146.5 0.0 copy-start.2
  146.5 0.0 copy-start.12
  146.5 3.5 %fusion.1 = f32[384,1024]{1,0:T(8,128)S(1)} fusion(bf16[384,4096]{1,0:T(8,128)(2,1)S(1)} %get-tuple-element.15, bf16[4096,1024]{1,0:T(8,128)(2,1)S(1)} %get-tuple-element.16), kind=kOutput, calls=%fused_computation.10 | convolution fusion | flops 3221225472 | bytes 13107200 | tf_op jit(solution)/shard_map/dot_general | solution.py:738
  150.1 0.0 copy-done.2
  150.1 0.0 copy-done.12
  150.1 1.5 %add_convert_fusion = bf16[384,1024]{1,0:T(8,128)(2,1)} fusion(f32[384,1024]{1,0:T(8,128)S(1)} %fusion.1, bf16[512,1024]{1,0:T(8,128)(2,1)S(1)} %copy-done.2, s32[384]{0:T(512)S(1)} %copy-done.12), kind=kOutput, calls=%fused_computation | convolution fusion | flops 403636224 | bytes 3409408 | tf_op jit(solution)/shard_map/dot_general | solution.py:737
  (4 shorter events, 0.0 us)
Async XLA Ops:
  0.0 2.0 %copy-start = (f32[3,3,1024]{2,1,0:T(4,128)S(1)}, f32[3,3,1024]{2,1,0:T(4,128)}, u32[]{:S(2)}) copy-start(f32[3,3,1024]{2,1,0:T(4,128)} %param.17) | copy-start | bytes 110596
  3.9 1.2 copy-start.1
  5.2 1.2 copy-start.6
  6.4 1.2 copy-start.7
  7.6 1.2 copy-start.8
  8.8 0.7 copy-start.11
  52.2 2.0 %copy-start.3 = (bf16[4,512,1024]{2,1,0:T(8,128)(2,1)}, bf16[4,512,1024]{2,1,0:T(8,128)(2,1)S(1)}, u32[]{:S(2)}) copy-start(bf16[4,512,1024]{2,1,0:T(8,128)(2,1)S(1)} %get-tuple-element.13.table_ref) | copy-start | bytes 12582916
  54.2 1.7 %copy-start.4 = (bf16[4096,384]{1,0:T(8,128)(2,1)}, bf16[4096,384]{1,0:T(8,128)(2,1)S(1)}, u32[]{:S(2)}) copy-start(bf16[4096,384]{1,0:T(8,128)(2,1)S(1)} %get-tuple-element.14.w_ref) | copy-start | bytes 9437188
  55.9 0.6 copy-start.10
  59.4 22.5 %copy-start.9 = (bf16[512,1024]{1,0:T(8,128)(2,1)S(1)}, bf16[512,1024]{1,0:T(8,128)(2,1)}, u32[]{:S(2)}) copy-start(bf16[512,1024]{1,0:T(8,128)(2,1)} %refs_1_.1) | copy-start | bytes 3145732
  81.9 1.1 copy-start.5
  146.5 3.6 %copy-start.2 = (bf16[512,1024]{1,0:T(8,128)(2,1)S(1)}, bf16[512,1024]{1,0:T(8,128)(2,1)}, u32[]{:S(2)}) copy-start(bf16[512,1024]{1,0:T(8,128)(2,1)} %refs_2_.1) | copy-start | bytes 3145732
  146.5 3.6 %copy-start.12 = (s32[384]{0:T(512)S(1)}, s32[384]{0:T(512)}, u32[]{:S(2)}) copy-start(s32[384]{0:T(512)} %param.11) | copy-start | bytes 4612

commit v2 on v1

--- a/solution.py
+++ b/solution.py
@@ -11,7 +11,7 @@
 MESH = pl.DeviceIdType.MESH
 LANES = 128
 SUBLANES = 8
-VMEM_BYTES = 56 << 20
+VMEM_BYTES = 36 << 20
 
 
 def shifted(value, axis, steps):
@@ -363,12 +363,13 @@
             dma((6,)),
         ],
         compiler_params=pltpu.CompilerParams(
-            collective_id=0, has_side_effects=True, vmem_limit_bytes=8 << 20
+            collective_id=0, has_side_effects=True, vmem_limit_bytes=56 << 20
         ),
     )(ids, gain, table, w_query, w_key, w_value)
 
 
 def mix_kernel(
+    me_ref,
     ids_ref,
     gain_ref,
     table_ref,
@@ -385,9 +386,10 @@
     n_dp, vocab, width = table_ref.shape
     features = n_dp * width
     taps = filt_ref.shape[0]
-    modes = rate_ref.shape[0]
+    modes = rate_ref.shape[1]
     segments, steps, lanes = out_ref.shape
-    lead = proj.shape[0] - segments * steps
+    lead = proj.shape[1] - segments * steps
+    mine = pl.ds(pl.multiple_of(me_ref[0] * lanes, lanes), lanes)
     total = jnp.zeros((vocab, 1), jnp.float32)
     for b in range(n_dp):
         block = table_ref[b].astype(jnp.float32)
@@ -396,30 +398,50 @@
     rows = jnp.zeros((vocab, 3 * lanes), jnp.float32)
     for b in range(n_dp):
         block = table_ref[b].astype(jnp.float32)
-        normed = (block * scale * gain_ref[:, b * width : (b + 1) * width]).astype(jnp.bfloat16)
+        gain = jnp.concatenate([gain_ref[b, r : r + 1, :] for r in range(width // lanes)], axis=1)
+        normed = (block * scale * gain).astype(jnp.bfloat16)
         rows = rows + jnp.dot(
             normed, w_ref[b * width : (b + 1) * width, :], preferred_element_type=jnp.float32
         )
     rows = rows.astype(jnp.bfloat16)
-    size = lead
-
-    def place(n, carry):
-        here = pl.ds(pl.multiple_of(n * size, size), size)
-        names = lax.broadcasted_iota(jnp.int32, (size, vocab), 1)
-        one_hot = (ids_ref[here, :] == names).astype(jnp.float32).astype(jnp.bfloat16)
-        proj[here, :] = jnp.dot(one_hot, rows, preferred_element_type=jnp.float32)
-        return carry
-
-    lax.fori_loop(0, proj.shape[0] // size, place, 0)
+    pieces = steps // lanes
+    per_segment = ids_ref.shape[1]
+    names = lax.broadcasted_iota(jnp.int32, (lanes, vocab), 1)
+    for s in range(segments):
+        by_lane = ids_ref[s].astype(jnp.float32)
+        square = jnp.concatenate(
+            [by_lane, jnp.zeros((lanes - per_segment, lanes), jnp.float32)], axis=0
+        )
+        columns = square.T.astype(jnp.int32)
+        one_hot = jnp.concatenate(
+            [
+                (columns[:, p : p + 1] == names).astype(jnp.float32).astype(jnp.bfloat16)
+                for p in range(pieces)
+            ],
+            axis=0,
+        )
+        picked = jnp.dot(one_hot, rows, preferred_element_type=jnp.float32)
+        for w in range(3):
+            proj[w, pl.ds(lead + s, steps, stride=segments), :] = picked[:, w * lanes : (w + 1) * lanes]
+    place_of = lax.broadcasted_iota(jnp.int32, (segments, lanes), 0)
+
+    def later(value, by):
+        return jnp.where(place_of >= by, pltpu.roll(value, by, 0), 0.0)
+
+    end = proj.shape[1]
+    for tap in range(1, taps):
+        for w in range(3):
+            tail = proj[w, end - tap * segments : end - (tap - 1) * segments, :]
+            proj[w, lead - tap * segments : lead - (tap - 1) * segments, :] = later(tail, 1)
+    size = lanes
 
     def convolve(n, carry):
         start = n * size + lead
         conv = [jnp.zeros((size, lanes), jnp.float32) for _ in range(3)]
         for tap in range(taps):
             here = pl.ds(pl.multiple_of(start - tap * segments, segments), size)
-            piece = proj[here, :]
             for w in range(3):
-                conv[w] = conv[w] + filt_ref[tap, w : w + 1, :] * piece[:, w * lanes : (w + 1) * lanes]
+                conv[w] = conv[w] + filt_ref[tap, w : w + 1, mine] * proj[w, here, :]
         there = pl.ds(pl.multiple_of(n * size, size), size)
         query[there, :] = conv[0]
         gated[there, :] = conv[1] * conv[2]
@@ -430,7 +452,12 @@
     def spread_rows(row):
         return jnp.broadcast_to(row, (segments, lanes))
 
-    decay = [spread_rows(jnp.exp(-rate_ref[m : m + 1, :])) for m in range(modes)]
+    def turned(ref):
+        value = ref[mine, :]
+        return jnp.concatenate([value, jnp.zeros((lanes, lanes - modes), jnp.float32)], axis=1).T
+
+    rate, residue = turned(rate_ref), turned(residue_ref)
+    decay = [spread_rows(jnp.exp(-rate[m : m + 1, :])) for m in range(modes)]
     unroll = 4
 
     def ends(n, state):
@@ -441,37 +468,33 @@
 
     zero = jnp.zeros((segments, lanes), jnp.float32)
     state = lax.fori_loop(0, steps // unroll, ends, (zero,) * modes)
-    place_of = lax.broadcasted_iota(jnp.int32, (segments, lanes), 0)
-
-    def later(value, by):
-        return jnp.where(place_of >= by, pltpu.roll(value, by, 0), 0.0)
-
     entering = []
     for m in range(modes):
         value = later(state[m], 1)
         by = 1
         while by < segments:
-            jump = jnp.exp(-rate_ref[m : m + 1, :] * float(steps * by))
+            jump = jnp.exp(-rate[m : m + 1, :] * float(steps * by))
             value = value + jump * later(value, by)
             by *= 2
         entering.append(value)
     strength = [
-        spread_rows(residue_ref[m : m + 1, :] * jnp.sqrt(2.0 * rate_ref[m : m + 1, :]))
-        for m in range(modes)
+        spread_rows(residue[m : m + 1, :] * jnp.sqrt(2.0 * rate[m : m + 1, :])) for m in range(modes)
     ]
-    skip = spread_rows(skip_ref[...])
+    skip = spread_rows(skip_ref[:, mine])
 
     def advance(n, state):
         for u in range(unroll):
             here = pl.ds(pl.multiple_of((n * unroll + u) * segments, segments), segments)
             row = gated[here, :]
-            state = tuple(d * s + row for d, s in zip(decay, state))
-            terms = [c * s for c, s in zip(strength, state)]
-            while len(terms) > 1:
-                terms = [a + b for a, b in zip(terms[::2], terms[1::2])] + (
-                    [terms[-1]] if len(terms) % 2 else []
-                )
-            query[here, :] = query[here, :] * (terms[0] + skip * row)
+            sums = [skip * row, None]
+            new = []
+            for m in range(modes):
+                now = decay[m] * state[m] + row
+                new.append(now)
+                term = strength[m] * now
+                sums[m % 2] = term if sums[m % 2] is None else sums[m % 2] + term
+            state = tuple(new)
+            query[here, :] = query[here, :] * (sums[0] + sums[1])
         return state
 
     lax.fori_loop(0, steps // unroll, advance, tuple(entering))
@@ -479,23 +502,23 @@
         out_ref[s] = query[pl.ds(s, steps, stride=segments), :].astype(jnp.bfloat16)
 
 
-def mix(ids, gain, table, w, filt, rate, residue, skip, segments, steps):
+def mix(me, ids, gain, table, w, filt, rate, residue, skip, segments, steps):
     whole = pl.BlockSpec(memory_space=pltpu.VMEM)
-    wide = w.shape[1]
-    lanes = wide // 3
+    lanes = w.shape[1] // 3
+    lead = segments * (filt.shape[0] - 1)
     return pl.pallas_call(
         mix_kernel,
         name="mix",
         out_shape=jax.ShapeDtypeStruct((segments, steps, lanes), jnp.bfloat16),
-        in_specs=[whole] * 8,
+        in_specs=[pl.BlockSpec(memory_space=pltpu.SMEM)] + [whole] * 8,
         out_specs=whole,
         scratch_shapes=[
-            pltpu.VMEM((ids.shape[0], wide), jnp.float32),
+            pltpu.VMEM((3, lead + segments * steps, lanes), jnp.float32),
             pltpu.VMEM((segments * steps, lanes), jnp.float32),
             pltpu.VMEM((segments * steps, lanes), jnp.float32),
         ],
         compiler_params=pltpu.CompilerParams(vmem_limit_bytes=VMEM_BYTES),
-    )(ids, gain, table, w, filt, rate, residue, skip)
+    )(me, ids, gain, table, w, filt, rate, residue, skip)
 
 
 def collect_kernel(
@@ -574,8 +597,7 @@
         remote(weight_ref, block(me), w_send.at[1], w_recv.at[1], ctx=up),
         remote(weight_ref, block(me), w_send.at[2], w_recv.at[2], ctx=partner),
     ]
-    for copy in own:
-        copy.start()
+    own[2].start()
     for copy in into:
         copy.wait()
     out = [
@@ -587,6 +609,8 @@
     for d in range(1, n_ctx):
         recv(at, d)
         first_hop(d)
+    own[0].start()
+    own[1].start()
 
     for hop in range(1, n_dp):
         for d in range(n_ctx):
@@ -703,32 +727,22 @@
 ):
     vocab = embed_table.shape[0]
     tok_rows = ids.shape[0]
-    taps = short_filter.shape[0]
-    me = lax.axis_index("ctx")
     gain = norm_gain.astype(jnp.float32).reshape(-1, LANES)
+    by_lane = ids.reshape(-1, LANES)
+    by_lane = jnp.pad(by_lane, ((0, -by_lane.shape[0] % SUBLANES), (0, 0)))
     all_ids, all_gain, all_table, w_mine = spread(
-        n_ctx, n_dp, ids.reshape(-1, LANES), gain, embed_table, w_query, w_key, w_value
-    )
-    all_gain = all_gain.reshape(1, -1)
-    by_step = all_ids.reshape(n_ctx, tok_rows)
-    before = jnp.concatenate(
-        [jnp.full((1, taps - 1), -1, jnp.int32), by_step[:-1, tok_rows - (taps - 1) :]], axis=0
-    )
-    pad = jnp.full((LANES - n_ctx * (taps - 1),), -1, jnp.int32)
-    ordered = jnp.concatenate([pad, before.T.reshape(-1), by_step.T.reshape(-1)])[:, None]
-
-    def mine(value, axis):
-        return lax.dynamic_slice_in_dim(value, me * LANES, LANES, axis)
-
+        n_ctx, n_dp, by_lane, gain, embed_table, w_query, w_key, w_value
+    )
     mixed = mix(
-        ordered,
+        lax.axis_index("ctx").astype(jnp.int32).reshape(1),
+        all_ids,
         all_gain,
         all_table,
         w_mine,
-        mine(short_filter, 2),
-        mine(pole_rate, 0).T,
-        mine(residue, 0).T,
-        mine(skip_gain, 0)[None, :],
+        short_filter,
+        pole_rate,
+        residue,
+        skip_gain[None, :],
         n_ctx,
         tok_rows,
     )

time: 152 us -> 136 us (0.89)
  Pallas kernels: 129 us -> 120 us
  local copies, waits for them, and re-layouts: 17.1 us -> 8.91 us
    pallas_call x1, Pallas kernels: 22.5 us -> 13.2 us  [mix(): pl.pallas_call(mix_kernel, name='mix', out_shape=jax.ShapeDtypeStruct((se...]
    broadcast_in_dim x3 -> x0, local copies, waits for them, and re-layouts: 3.66 us -> none  [the longest x1 2.31 us: by_channel(): jnp.concatenate([pad, before.T.reshape(-1), by_step.T.reshape(-1)])[:, None]]
    unnamed x28 -> x20, local copies, waits for them, and re-layouts: 11 us -> 7.64 us
    transpose x4 -> x0, local copies, waits for them, and re-layouts: 1.54 us -> none  [the longest x1 1.32 us: by_channel(): mine(residue, 0)]
where the time goes in v2:
time: 136 us; the launch traced here: 135 us
  Pallas kernels  120 us (88%)
  local copies, waits for them, and re-layouts  8.91 us (7%)
  matrix products  4.91 us (4%)
    pallas_call x1, Pallas kernels, collect(): pl.pallas_call(lambda *refs: collect_kernel(n_ctx, n_dp, *refs), name='co...  63.6 us
    pallas_call x1, Pallas kernels, spread(): pl.pallas_call(lambda *refs: spread_kernel(n_ctx, n_dp, *refs), name='spr...  43.5 us
    pallas_call x1, Pallas kernels, mix(): pl.pallas_call(mix_kernel, name='mix', out_shape=jax.ShapeDtypeStruct((se...  13.2 us
    unnamed x20, local copies, waits for them, and re-layouts  7.64 us
    dot_general x1, matrix products, by_channel(): output = jnp.dot(all_mixed, all_rows, preferred_element_type=jnp.float32)  3.4 us

profile of v2, /device:TPU:0, one launch (start us, length us, event | category | flops | bytes accessed | tf_op | source)
XLA Modules:
  0.0 135.4 jit_solution(6219678696521243994)
XLA Ops:
  0.0 0.0 copy-start.6
  0.0 0.0 copy-start.3
  0.0 1.3 bitcast_convert_fusion.refs_1_
  1.3 1.3 pad.4.refs_0_
  2.6 1.0 copy.12.rate_ref
  3.6 1.0 copy.13.residue_ref
  4.7 43.5 %spread.1 = (s32[8,8,128]{2,1,0:T(8,128)}, f32[4,8,128]{2,1,0:T(8,128)}, bf16[4,512,1024]{2,1,0:T(8,128)(2,1)}, bf16[4096,384]{1,0:T(8,128)(2,1)}) custom-call(s32[8,128]{1,0:T(8,128)} %pad.4.refs_0_, f32[8,128]{1,0:T(8,128)} %bitcast_convert_fusion.refs_1_, bf16[512,1024]{1,0:T(8,128)(2,1)} %refs_2_.1, bf16[512,1024]{1,0:T(8,128)(2,1)} %refs_3_.1, ...), custom_call_target="tpu_custom_call" | custom-call | tf_op jit(solution)/shard_map/spread/pallas_call | solution.py:339
  48.1 0.0 copy-done.6
  48.1 0.0 copy-done.3
  48.1 0.0 copy-start
  48.1 2.2 %copy-done = bf16[4,512,1024]{2,1,0:T(8,128)(2,1)S(1)} copy-done((bf16[4,512,1024]{2,1,0:T(8,128)(2,1)S(1)}, bf16[4,512,1024]{2,1,0:T(8,128)(2,1)}, u32[]{:S(2)}) %copy-start) | copy-done | bytes 4194328
  50.3 0.0 copy-start.1
  50.3 1.9 %copy-done.1 = bf16[4096,384]{1,0:T(8,128)(2,1)S(1)} copy-done((bf16[4096,384]{1,0:T(8,128)(2,1)S(1)}, bf16[4096,384]{1,0:T(8,128)(2,1)}, u32[]{:S(2)}) %copy-start.1) | copy-done | bytes 3145752
  52.2 0.0 copy-start.4
  52.2 0.8 copy-done.4
  53.0 0.0 copy-start.5
  53.0 0.7 copy-done.5
  53.7 0.0 copy-start.2
  53.7 13.2 %mix.1.refs_0_ = bf16[8,384,128]{2,1,0:T(8,128)(2,1)S(1)} custom-call(s32[1]{0:T(128)} %bitcast.me_ref, s32[8,8,128]{2,1,0:T(8,128)S(1)} %copy-done.4, f32[4,8,128]{2,1,0:T(8,128)S(1)} %copy-done.5, bf16[4,512,1024]{2,1,0:T(8,128)(2,1)S(1)} %copy-done, bf16[4096,384]{1,0:T(8,128)(2,1)S(1)} %copy-done.1, f32[3,3,1024]{2,1,0:T(4,128)S(1)} %copy-done.3, ...), custom_call_target="tpu_custom_call" | custom-call | tf_op jit(solution)/shard_map/mix/pallas_call | solution.py:509
  66.9 0.0 copy-done.2
  66.9 63.6 %collect.1 = (bf16[384,4096]{1,0:T(8,128)(2,1)S(1)}, bf16[4096,1024]{1,0:T(8,128)(2,1)S(1)}) custom-call(bf16[8,384,128]{2,1,0:T(8,128)(2,1)S(1)} %mix.1.refs_0_, bf16[512,1024]{1,0:T(8,128)(2,1)S(1)} %copy-done.2), custom_call_target="tpu_custom_call" | custom-call | tf_op jit(solution)/shard_map/collect/pallas_call | solution.py:686
  130.4 0.0 copy-start.7
  130.4 0.0 copy-start.8
  130.4 3.4 %fusion.1 = f32[384,1024]{1,0:T(8,128)S(1)} fusion(bf16[384,4096]{1,0:T(8,128)(2,1)S(1)} %get-tuple-element.15, bf16[4096,1024]{1,0:T(8,128)(2,1)S(1)} %get-tuple-element.16), kind=kOutput, calls=%fused_computation.4 | convolution fusion | flops 3221225472 | bytes 13107200 | tf_op jit(solution)/shard_map/dot_general | solution.py:752
  133.9 0.0 copy-done.7
  133.9 0.0 copy-done.8
  133.9 1.5 %add_convert_fusion = bf16[384,1024]{1,0:T(8,128)(2,1)} fusion(f32[384,1024]{1,0:T(8,128)S(1)} %fusion.1, bf16[512,1024]{1,0:T(8,128)(2,1)S(1)} %copy-done.7, s32[384]{0:T(512)S(1)} %copy-done.8), kind=kOutput, calls=%fused_computation | convolution fusion | flops 403636224 | bytes 3409408 | tf_op jit(solution)/shard_map/dot_general | solution.py:751
Async XLA Ops:
  0.0 48.1 %copy-start.6 = (f32[1024]{0:T(1024)S(1)}, f32[1024]{0:T(1024)}, u32[]{:S(2)}) copy-start(f32[1024]{0:T(1024)} %param.20) | copy-start | bytes 12292
  0.0 48.1 %copy-start.3 = (f32[3,3,1024]{2,1,0:T(4,128)S(1)}, f32[3,3,1024]{2,1,0:T(4,128)}, u32[]{:S(2)}) copy-start(f32[3,3,1024]{2,1,0:T(4,128)} %filt_ref.1) | copy-start | bytes 110596
  48.1 2.2 %copy-start = (bf16[4,512,1024]{2,1,0:T(8,128)(2,1)S(1)}, bf16[4,512,1024]{2,1,0:T(8,128)(2,1)}, u32[]{:S(2)}) copy-start(bf16[4,512,1024]{2,1,0:T(8,128)(2,1)} %get-tuple-element.13.table_ref) | copy-start | bytes 12582916
  50.3 1.9 %copy-start.1 = (bf16[4096,384]{1,0:T(8,128)(2,1)S(1)}, bf16[4096,384]{1,0:T(8,128)(2,1)}, u32[]{:S(2)}) copy-start(bf16[4096,384]{1,0:T(8,128)(2,1)} %get-tuple-element.14.w_ref) | copy-start | bytes 9437188
  52.2 0.8 copy-start.4
  53.0 0.7 copy-start.5
  53.7 13.2 %copy-start.2 = (bf16[512,1024]{1,0:T(8,128)(2,1)S(1)}, bf16[512,1024]{1,0:T(8,128)(2,1)}, u32[]{:S(2)}) copy-start(bf16[512,1024]{1,0:T(8,128)(2,1)} %refs_1_.1) | copy-start | bytes 3145732
  130.4 3.4 %copy-start.7 = (bf16[512,1024]{1,0:T(8,128)(2,1)S(1)}, bf16[512,1024]{1,0:T(8,128)(2,1)}, u32[]{:S(2)}) copy-start(bf16[512,1024]{1,0:T(8,128)(2,1)} %refs_2_.1) | copy-start | bytes 3145732
  130.4 3.4 %copy-start.8 = (s32[384]{0:T(512)S(1)}, s32[384]{0:T(512)}, u32[]{:S(2)}) copy-start(s32[384]{0:T(512)} %param.11) | copy-start | bytes 4612

commit v3 on v2

--- a/solution.py
+++ b/solution.py
@@ -333,7 +333,7 @@
 
 def spread(n_ctx, n_dp, ids, gain, table, w_query, w_key, w_value):
     depth, wide = w_query.shape[0], w_query.shape[1] // n_ctx
-    chunks = 2
+    chunks = 4
     anywhere = pl.BlockSpec(memory_space=pl.ANY)
     dma = pltpu.SemaphoreType.DMA
     return pl.pallas_call(
@@ -363,7 +363,7 @@
             dma((6,)),
         ],
         compiler_params=pltpu.CompilerParams(
-            collective_id=0, has_side_effects=True, vmem_limit_bytes=56 << 20
+            collective_id=0, has_side_effects=True, vmem_limit_bytes=53 << 20
         ),
     )(ids, gain, table, w_query, w_key, w_value)
 

time: 136 us -> 133 us (0.978)
  local copies, waits for them, and re-layouts: 8.91 us -> 6.85 us
    unnamed x20 -> x16, local copies, waits for them, and re-layouts: 7.64 us -> 6.16 us
where the time goes in v3:
time: 133 us
  Pallas kernels  120 us (90%)
  local copies, waits for them, and re-layouts  6.85 us (5%)
  matrix products  4.91 us (4%)
    pallas_call x1, Pallas kernels, collect(): pl.pallas_call(lambda *refs: collect_kernel(n_ctx, n_dp, *refs), name='co...  63.6 us
    pallas_call x1, Pallas kernels, spread(): pl.pallas_call(lambda *refs: spread_kernel(n_ctx, n_dp, *refs), name='spr...  43.6 us
    pallas_call x1, Pallas kernels, mix(): pl.pallas_call(mix_kernel, name='mix', out_shape=jax.ShapeDtypeStruct((se...  13.2 us
    unnamed x16, local copies, waits for them, and re-layouts  6.16 us
    dot_general x1, matrix products, by_channel(): output = jnp.dot(all_mixed, all_rows, preferred_element_type=jnp.float32)  3.4 us

profile of v3, /device:TPU:0, one launch (start us, length us, event | category | flops | bytes accessed | tf_op | source)
XLA Modules:
  0.0 132.9 jit_solution(10937560530718124280)
XLA Ops:
  0.0 0.0 copy-start.4
  0.0 0.0 copy-start.3
  0.0 0.7 bitcast_convert_fusion.refs_1_
  0.7 0.7 pad.4.refs_0_
  1.4 1.0 copy.12.rate_ref
  2.4 1.0 copy.13.residue_ref
  3.5 43.6 %spread.1 = (s32[8,8,128]{2,1,0:T(8,128)S(1)}, f32[4,8,128]{2,1,0:T(8,128)S(1)}, bf16[4,512,1024]{2,1,0:T(8,128)(2,1)}, bf16[4096,384]{1,0:T(8,128)(2,1)}) custom-call(s32[8,128]{1,0:T(8,128)S(1)} %pad.4.refs_0_, f32[8,128]{1,0:T(8,128)S(1)} %bitcast_convert_fusion.refs_1_, bf16[512,1024]{1,0:T(8,128)(2,1)} %refs_2_.1, bf16[512,1024]{1,0:T(8,128)(2,1)} %refs_3_.1, ...), custom_call_target="tpu_custom_call" | custom-call | tf_op jit(solution)/shard_map/spread/pallas_call | solution.py:339
  47.1 0.0 copy-done.4
  47.1 0.0 copy-done.3
  47.1 0.0 copy-start
  47.1 2.2 %copy-done = bf16[4,512,1024]{2,1,0:T(8,128)(2,1)S(1)} copy-done((bf16[4,512,1024]{2,1,0:T(8,128)(2,1)S(1)}, bf16[4,512,1024]{2,1,0:T(8,128)(2,1)}, u32[]{:S(2)}) %copy-start) | copy-done | bytes 4194328
  49.3 0.0 copy-start.1
  49.3 1.9 %copy-done.1 = bf16[4096,384]{1,0:T(8,128)(2,1)S(1)} copy-done((bf16[4096,384]{1,0:T(8,128)(2,1)S(1)}, bf16[4096,384]{1,0:T(8,128)(2,1)}, u32[]{:S(2)}) %copy-start.1) | copy-done | bytes 3145752
  51.2 0.0 copy-start.2
  51.2 13.2 %mix.1.refs_0_ = bf16[8,384,128]{2,1,0:T(8,128)(2,1)S(1)} custom-call(s32[1]{0:T(128)} %bitcast.me_ref, s32[8,8,128]{2,1,0:T(8,128)S(1)} %get-tuple-element.11.ids_ref, f32[4,8,128]{2,1,0:T(8,128)S(1)} %get-tuple-element.12.gain_ref, bf16[4,512,1024]{2,1,0:T(8,128)(2,1)S(1)} %copy-done, bf16[4096,384]{1,0:T(8,128)(2,1)S(1)} %copy-done.1, ...), custom_call_target="tpu_custom_call" | custom-call | tf_op jit(solution)/shard_map/mix/pallas_call | solution.py:509
  64.3 0.0 copy-done.2
  64.4 63.6 %collect.1 = (bf16[384,4096]{1,0:T(8,128)(2,1)S(1)}, bf16[4096,1024]{1,0:T(8,128)(2,1)S(1)}) custom-call(bf16[8,384,128]{2,1,0:T(8,128)(2,1)S(1)} %mix.1.refs_0_, bf16[512,1024]{1,0:T(8,128)(2,1)S(1)} %copy-done.2), custom_call_target="tpu_custom_call" | custom-call | tf_op jit(solution)/shard_map/collect/pallas_call | solution.py:686
  128.0 0.0 copy-start.5
  128.0 0.0 copy-start.6
  128.0 3.4 %fusion.1 = f32[384,1024]{1,0:T(8,128)S(1)} fusion(bf16[384,4096]{1,0:T(8,128)(2,1)S(1)} %get-tuple-element.15, bf16[4096,1024]{1,0:T(8,128)(2,1)S(1)} %get-tuple-element.16), kind=kOutput, calls=%fused_computation.4 | convolution fusion | flops 3221225472 | bytes 13107200 | tf_op jit(solution)/shard_map/dot_general | solution.py:752
  131.4 0.0 copy-done.5
  131.4 0.0 copy-done.6
  131.4 1.5 %add_convert_fusion = bf16[384,1024]{1,0:T(8,128)(2,1)} fusion(f32[384,1024]{1,0:T(8,128)S(1)} %fusion.1, bf16[512,1024]{1,0:T(8,128)(2,1)S(1)} %copy-done.5, s32[384]{0:T(512)S(1)} %copy-done.6), kind=kOutput, calls=%fused_computation | convolution fusion | flops 403636224 | bytes 3409408 | tf_op jit(solution)/shard_map/dot_general | solution.py:751
Async XLA Ops:
  0.0 47.1 %copy-start.4 = (f32[1024]{0:T(1024)S(1)}, f32[1024]{0:T(1024)}, u32[]{:S(2)}) copy-start(f32[1024]{0:T(1024)} %param.20) | copy-start | bytes 12292
  0.0 47.1 %copy-start.3 = (f32[3,3,1024]{2,1,0:T(4,128)S(1)}, f32[3,3,1024]{2,1,0:T(4,128)}, u32[]{:S(2)}) copy-start(f32[3,3,1024]{2,1,0:T(4,128)} %filt_ref.1) | copy-start | bytes 110596
  47.1 2.2 %copy-start = (bf16[4,512,1024]{2,1,0:T(8,128)(2,1)S(1)}, bf16[4,512,1024]{2,1,0:T(8,128)(2,1)}, u32[]{:S(2)}) copy-start(bf16[4,512,1024]{2,1,0:T(8,128)(2,1)} %get-tuple-element.13.table_ref) | copy-start | bytes 12582916
  49.3 1.9 %copy-start.1 = (bf16[4096,384]{1,0:T(8,128)(2,1)S(1)}, bf16[4096,384]{1,0:T(8,128)(2,1)}, u32[]{:S(2)}) copy-start(bf16[4096,384]{1,0:T(8,128)(2,1)} %get-tuple-element.14.w_ref) | copy-start | bytes 9437188
  51.2 13.2 %copy-start.2 = (bf16[512,1024]{1,0:T(8,128)(2,1)S(1)}, bf16[512,1024]{1,0:T(8,128)(2,1)}, u32[]{:S(2)}) copy-start(bf16[512,1024]{1,0:T(8,128)(2,1)} %refs_1_.1) | copy-start | bytes 3145732
  128.0 3.4 %copy-start.5 = (bf16[512,1024]{1,0:T(8,128)(2,1)S(1)}, bf16[512,1024]{1,0:T(8,128)(2,1)}, u32[]{:S(2)}) copy-start(bf16[512,1024]{1,0:T(8,128)(2,1)} %refs_2_.1) | copy-start | bytes 3145732
  128.0 3.4 %copy-start.6 = (s32[384]{0:T(512)S(1)}, s32[384]{0:T(512)}, u32[]{:S(2)}) copy-start(s32[384]{0:T(512)} %param.11) | copy-start | bytes 4612
